TPU v7x, 128 devices: a whole 4x4x4 slice. The times are simulated.
128 devices in a mesh: freq: 4 (over z_hi, core), vis: 32 (over z_lo, y, x).
Axes of the slice: x: 4, y: 4, z: 4 (z_hi: 2, z_lo: 2; z = z_hi * 2 + z_lo), core: 2. Of those that a mesh axis runs over, the one named last changes fastest.
Arguments:
- model_input: bfloat16 [2, 16, 512, 512], P(None, 'freq', 'vis'), parts along dimension 1, may hold values from -6 to 6
- w_kernels: bfloat16 [64, 2, 128, 128], P('freq'), parts along dimension 0, may hold values from -0.375 to 0.375
- visibilities: bfloat16 [4096, 2, 128, 128], P(('freq', 'vis')), parts along dimension 0, may hold values from -6 to 6
- tile_facet: int32 [4096], P(('freq', 'vis')), parts along dimension 0, may hold values from 0 to 3
- tile_patch: int32 [4096], P(('freq', 'vis')), parts along dimension 0, may hold values from 0 to 15
- tile_wplane: int32 [4096], P(('freq', 'vis')), parts along dimension 0, may hold values from 0 to 15
- tile_count: int32 [128], P(('freq', 'vis')), parts along dimension 0, may hold values from 16 to 32, as said below
Outputs:
- residual_image: float32 [16, 512, 512], P('freq', 'vis'), parts along dimension 0
There are 4 independent parts, one for each index of `freq`. A program takes and returns all parts, laid end to end along the dimension named above; each array names one. Nothing has to cross between parts.
Inputs may be any that keep to these rules, and one draw needn't show every extreme that they name: `tile_count`: each device's live tiles fill its first slots; some device holds exactly 32.
All inputs are finite; a program needn't handle non-finite values.
Results may differ from a plain program's by a relative error of at most 0.02.
Values may be sent and summed in bfloat16 or wider, within the bound.
A program may use at most 128 MiB of HBM per device.

v0:
```python
import math
import jax
import jax.numpy as jnp
from jax import lax
from jax.sharding import PartitionSpec as P

P_SIZE = 512
S = 128
F = 4
WPLANES = 16
CYCLES = 2
TILE_CAP = 32
NP = 16
loop_gain = 0.5


def dft_tables(first_row, row_count, length):
    row_ids = first_row + jnp.arange(row_count, dtype=jnp.int32)
    col_ids = jnp.arange(length, dtype=jnp.int32)
    phases = row_ids[:, None] * col_ids[None, :] % length
    angles = phases.astype(jnp.float32) * (2.0 * math.pi / length)
    scaling = 1.0 / math.sqrt(length)
    return (jnp.cos(angles) * scaling, jnp.sin(angles) * scaling)


def lowprec(pattern, first_op, second_op):
    return jnp.einsum(pattern, first_op, second_op, preferred_element_type=jnp.float32)


def exact(pattern, first_op, second_op):
    return jnp.einsum(
        pattern,
        first_op,
        second_op,
        precision=lax.Precision.HIGHEST,
        preferred_element_type=jnp.float32,
    )


def column_pass(half_grid, cosine_half, sine_half):
    half_real, half_imag = (half_grid[:, 0], half_grid[:, 1])
    grid_real = lowprec("ij,fjk->fik", cosine_half, half_real) + lowprec(
        "ij,fjk->fik", sine_half, half_imag
    )
    grid_imag = lowprec("ij,fjk->fik", cosine_half, half_imag) - lowprec(
        "ij,fjk->fik", sine_half, half_real
    )
    return jnp.stack([grid_real, grid_imag], axis=1).astype(jnp.bfloat16)


def tile_terms(patches, kernel, observed, alive):
    patch_real, patch_imag = (patches[:, 0], patches[:, 1])
    kern_real, kern_imag = (kernel[:, 0], kernel[:, 1])
    mid_real = (
        lowprec("tij,tjk->tik", kern_real, patch_real)
        - lowprec("tij,tjk->tik", kern_imag, patch_imag)
    ).astype(jnp.bfloat16)
    mid_imag = (
        lowprec("tij,tjk->tik", kern_real, patch_imag)
        + lowprec("tij,tjk->tik", kern_imag, patch_real)
    ).astype(jnp.bfloat16)
    model_real = lowprec("tij,tkj->tik", mid_real, kern_real) - lowprec(
        "tij,tkj->tik", mid_imag, kern_imag
    )
    model_imag = lowprec("tij,tkj->tik", mid_real, kern_imag) + lowprec(
        "tij,tkj->tik", mid_imag, kern_real
    )
    resid_real = ((observed[:, 0].astype(jnp.float32) - model_real) * alive[:, None, None]).astype(
        jnp.bfloat16
    )
    resid_imag = ((observed[:, 1].astype(jnp.float32) - model_imag) * alive[:, None, None]).astype(
        jnp.bfloat16
    )
    back_real = (
        lowprec("tji,tjk->tik", kern_real, resid_real)
        + lowprec("tji,tjk->tik", kern_imag, resid_imag)
    ).astype(jnp.bfloat16)
    back_imag = (
        lowprec("tji,tjk->tik", kern_real, resid_imag)
        - lowprec("tji,tjk->tik", kern_imag, resid_real)
    ).astype(jnp.bfloat16)
    out_real = lowprec("tij,tjk->tik", back_real, kern_real) + lowprec(
        "tij,tjk->tik", back_imag, kern_imag
    )
    out_imag = lowprec("tij,tjk->tik", back_imag, kern_real) - lowprec(
        "tij,tjk->tik", back_real, kern_imag
    )
    return jnp.stack([out_real, out_imag], axis=1).reshape(patches.shape[0], 2 * S * S)


def local(model_input, w_kernels, visibilities, tile_facet, tile_patch, tile_wplane, tile_count):
    devices = lax.axis_size("vis")
    position = lax.axis_index("vis")
    local_rows = P_SIZE // devices
    cosine_full, sine_full = dft_tables(0, P_SIZE, P_SIZE)
    cosine_half = cosine_full.astype(jnp.bfloat16)
    sine_half = sine_full.astype(jnp.bfloat16)
    weight = math.sqrt(F * NP / (TILE_CAP * devices))
    slots = tile_facet * NP + tile_patch
    alive = (jnp.arange(TILE_CAP, dtype=jnp.int32) < tile_count[0]).astype(jnp.float32)
    kernel_table = w_kernels.reshape(WPLANES, 2 * S * S)
    block_count = TILE_CAP // 16
    blocks = (
        slots.reshape(block_count, 16),
        tile_wplane.reshape(block_count, 16),
        visibilities.reshape(block_count, 16, 2, S, S),
        alive.reshape(block_count, 16),
    )
    residual_image = jnp.zeros((F, local_rows, P_SIZE), jnp.float32)
    for cycle_index in range(CYCLES):
        if cycle_index == 0:
            sky_model = model_input[0]
        else:
            sky_model = (
                model_input[cycle_index].astype(jnp.float32) + loop_gain * residual_image
            ).astype(jnp.bfloat16)
        half_real = lowprec("fij,jk->fik", sky_model, cosine_half)
        half_imag = -lowprec("fij,jk->fik", sky_model, sine_half)
        half_grid = jnp.stack([half_real, half_imag], axis=1).astype(jnp.bfloat16)
        column_half = lax.all_to_all(half_grid, "vis", split_axis=3, concat_axis=2, tiled=True)
        grid_part = column_pass(column_half, cosine_half, sine_half)
        full_grid = lax.all_gather(grid_part, "vis", axis=3, tiled=True)
        patch_table = (
            full_grid.reshape(F, 2, P_SIZE // S, S, P_SIZE // S, S)
            .transpose(0, 2, 4, 1, 3, 5)
            .reshape(F * NP, 2 * S * S)
        )

        def accumulate(running, tile_block):
            slot_ids, plane_ids, observed, live_block = tile_block
            choose = (slot_ids[:, None] == jnp.arange(F * NP, dtype=jnp.int32)[None, :]).astype(
                jnp.bfloat16
            )
            patches = (
                jnp.dot(choose, patch_table, preferred_element_type=jnp.float32)
                .astype(jnp.bfloat16)
                .reshape(16, 2, S, S)
            )
            plane_pick = (
                plane_ids[:, None] == jnp.arange(WPLANES, dtype=jnp.int32)[None, :]
            ).astype(jnp.bfloat16)
            kernel = (
                jnp.dot(plane_pick, kernel_table, preferred_element_type=jnp.float32)
                .astype(jnp.bfloat16)
                .reshape(16, 2, S, S)
            )
            tile_sums = tile_terms(patches, kernel, observed, live_block)
            return (running.at[slot_ids].add(tile_sums), None)

        summed, unused = lax.scan(accumulate, jnp.zeros((F * NP, 2 * S * S), jnp.float32), blocks)
        resid_grid = (
            summed.reshape(F, P_SIZE // S, P_SIZE // S, 2, S, S)
            .transpose(0, 3, 1, 4, 2, 5)
            .reshape(F, 2, P_SIZE, P_SIZE)
        )
        total_grid = lax.psum(resid_grid.astype(jnp.bfloat16), "vis").astype(jnp.float32)
        cosine_rows, sine_rows = dft_tables(position * local_rows, local_rows, P_SIZE)
        spec_real = exact("ij,fjk->fik", cosine_rows, total_grid[:, 0]) - exact(
            "ij,fjk->fik", sine_rows, total_grid[:, 1]
        )
        spec_imag = exact("ij,fjk->fik", cosine_rows, total_grid[:, 1]) + exact(
            "ij,fjk->fik", sine_rows, total_grid[:, 0]
        )
        residual_image = (
            exact("fij,jk->fik", spec_real, cosine_full)
            - exact("fij,jk->fik", spec_imag, sine_full)
        ) * weight
    return residual_image


def solution(mesh):
    return jax.shard_map(
        local,
        mesh=mesh,
        in_specs=(
            P(None, "freq", "vis", None),
            P("freq", None, None, None),
            P(("freq", "vis"), None, None, None),
            P(("freq", "vis")),
            P(("freq", "vis")),
            P(("freq", "vis")),
            P(("freq", "vis")),
        ),
        out_specs=P("freq", "vis", None),
        check_vma=False,
    )
```

profile of v0, /device:TPU:0, one launch (start us, length us, event | category | flops | bytes accessed | tf_op | source)
XLA Modules:
  0.0 1282.2 jit_solution(3081509541282992001)
XLA Ops:
  6.5 5.0 fusion.92
  11.6 4.2 fusion.95
  17.6 17.2 %all_to_all.36 = bf16[32,2,1024]{2,1,0:T(2,128)(2,1)S(1)} all-to-all(bf16[32,2,1024]{2,1,0:T(2,128)(2,1)S(1)} %reshape.173), channel_id=1, replica_groups=mesh['freq'=4,'vis'=32] {'vis'}, dimensions={0} | all-to-all | bytes 262144 | tf_op jit(solution)/shard_map/all_to_all | solution.py:120
  38.0 4.0 fusion.125
  42.0 4.0 fusion.127
  46.0 4.4 fusion.90
  50.4 4.2 fusion.91
  59.6 152.0 %all-gather.3.cloned.1.call-done = bf16[4,2,512,512]{2,3,0,1:T(8,128)(2,1)} async-done(((bf16[4,2,512,16]{2,3,0,1:T(8,128)(2,1)}), bf16[4,2,512,512]{2,3,0,1:T(8,128)(2,1)}) %all-gather.3.cloned.1.call-update) | async-done | bytes 4194320 | tf_op jit(solution)/shard_map/all_gather | solution.py:122
  211.6 7.0 reshape.138
  218.5 7.5 copy.83
  226.0 7.3 reshape.139
  233.3 3.9 broadcast.76.clone
  237.2 43.1 %while.20 = (s32[]{:T(128)}, f32[64,32768]{1,0:T(8,128)}, s32[2,16]{1,0:T(2,128)S(1)}, s32[2,16]{1,0:T(2,128)S(1)}, bf16[16,32768]{1,0:T(8,128)(2,1)S(1)}, /*ind...) while((s32[]{:T(128)}, f32[64,32768]{1,0:T(8,128)}, ...), condition=%wide.region_2.3_spmd, body=%wide.region_0.2_spmd.sunk | while | flops 1164969216 | bytes 89130760 | solution.py:150
  248.0 10.6 scatter_custom_fusion.9
  269.4 10.6 scatter_custom_fusion.9
  280.3 4.0 convert_bitcast_fusion.1
  285.6 5.9 copy.143
  291.5 7.2 convert_element_type.191
  298.7 4.4 copy.86
  303.2 321.4 %all-reduce.3.cloned.1.call-done = bf16[4,2,512,512]{3,2,0,1:T(8,128)(2,1)} async-done(((bf16[4,2,512,512]{3,2,0,1:T(8,128)(2,1)}), bf16[4,2,512,512]{3,2,0,1:T(8,128)(2,1)}) %all-reduce.3.cloned.1.call-update) | async-done | bytes 4194320 | tf_op jit(solution)/shard_map/psum | solution.py:156
  624.6 2.8 fusion.63
  627.3 2.7 fusion.78
  630.0 4.9 fusion.103
  637.1 4.7 fusion.81
  641.8 4.5 fusion.93
  646.3 4.5 fusion.94
  652.7 15.9 %all_to_all.37 = bf16[32,2,1024]{2,1,0:T(2,128)(2,1)S(1)} all-to-all(bf16[32,2,1024]{2,1,0:T(2,128)(2,1)S(1)} %reshape.175), channel_id=1, replica_groups=mesh['freq'=4,'vis'=32] {'vis'}, dimensions={0} | all-to-all | bytes 262144 | tf_op jit(solution)/shard_map/all_to_all | solution.py:120
  671.9 4.0 fusion.122
  675.8 4.0 fusion.120
  679.8 4.2 fusion.89
  684.0 4.2 fusion.88
  689.0 155.5 %all-gather.5.cloned.1.call-done = bf16[4,2,512,512]{2,3,0,1:T(8,128)(2,1)} async-done(((bf16[4,2,512,16]{2,3,0,1:T(8,128)(2,1)}), bf16[4,2,512,512]{2,3,0,1:T(8,128)(2,1)}) %all-gather.5.cloned.1.call-update) | async-done | bytes 4194320 | tf_op jit(solution)/shard_map/all_gather | solution.py:122
  844.4 7.1 reshape.140
  851.5 7.5 copy.92
  859.0 7.3 reshape.141
  866.3 3.9 broadcast.76
  870.2 42.9 %while.21 = (s32[]{:T(128)}, f32[64,32768]{1,0:T(8,128)}, s32[2,16]{1,0:T(2,128)S(1)}, s32[2,16]{1,0:T(2,128)S(1)}, bf16[16,32768]{1,0:T(8,128)(2,1)S(1)}, /*ind...) while((s32[]{:T(128)}, f32[64,32768]{1,0:T(8,128)}, ...), condition=%wide.region_6.7_spmd, body=%wide.region_4.6_spmd.sunk | while | flops 1164969216 | bytes 89130760 | solution.py:150
  881.0 10.6 scatter_custom_fusion.11
  902.3 10.6 scatter_custom_fusion.11
  913.1 4.1 convert_bitcast_fusion
  918.3 5.9 copy.142
  924.2 7.2 convert_element_type.197
  931.4 4.4 copy.95
  935.9 321.6 %all-reduce.5.cloned.1.call-done = bf16[4,2,512,512]{3,2,0,1:T(8,128)(2,1)} async-done(((bf16[4,2,512,512]{3,2,0,1:T(8,128)(2,1)}), bf16[4,2,512,512]{3,2,0,1:T(8,128)(2,1)}) %all-reduce.5.cloned.1.call-update) | async-done | bytes 4194320 | tf_op jit(solution)/shard_map/psum | solution.py:156
  1257.5 2.8 fusion.67
  1260.2 2.7 fusion.74
  1262.9 4.7 fusion.101
  1269.8 5.6 fusion.72
  (161 shorter events, 64.2 us)
Async XLA Ops:
  6.5 5.1 copy-start.5
  6.5 205.0 %all-gather.3.cloned.1.call-start = ((), (), s32[]{:S(2)}) async-start(), calls=%async_computation.2 | async-start | bytes 4325376 | tf_op jit(solution)/shard_map/all_gather | solution.py:122
  46.0 9.4 copy-start.4
  54.6 4.8 copy-start.6
  54.6 4.8 copy-start.7
  54.6 4.9 copy-start.8
  55.3 569.2 %all-reduce.3.cloned.1.call-start = ((), (), s32[]{:S(2)}) async-start(), calls=%async_computation.3 | async-start | bytes 8388608 | tf_op jit(solution)/shard_map/psum | solution.py:156
  237.2 2.2 copy-start.1
  258.6 2.2 copy-start.1
  303.1 541.3 %all-gather.5.cloned.1.call-start = ((), (), s32[]{:S(2)}) async-start(), calls=%async_computation.4 | async-start | bytes 4325376 | tf_op jit(solution)/shard_map/all_gather | solution.py:122
  624.6 10.4 copy-start.2
  688.9 568.6 %all-reduce.5.cloned.1.call-start = ((), (), s32[]{:S(2)}) async-start(), calls=%async_computation.5 | async-start | bytes 8388608 | tf_op jit(solution)/shard_map/psum | solution.py:156
  870.2 2.2 copy-start
  891.6 2.2 copy-start
  1257.5 10.2 copy-start.3
Sparse Core Ops, SparseCore 0:
  55.4 156.0 all-gather.2
  303.2 321.2 all-reduce.2
  689.0 155.3 all-gather.4
  936.0 321.3 all-reduce.4
where the time goes:
time: 1290 us; the launch traced here: 1280 us
  waiting for transfers between devices  950 us (74%)
  local copies, waits for them, and re-layouts  116 us (9%)
  matrix products  114 us (9%)
  other arithmetic  52.7 us (4%)
  blocking collectives  33.1 us (3%)
  between operations  14.4 us (1%)
    psum x2, waiting for transfers between devices, local(): lax.psum(resid_grid.astype(jnp.bfloat16), 'vis').astype(jnp.float32)  643 us
    all_gather x2, waiting for transfers between devices, local(): full_grid = lax.all_gather(grid_part, 'vis', axis=3, tiled=True)  307 us
    dot_general x76, matrix products, lowprec(): jnp.einsum(pattern, first_op, second_op, preferred_element_type=jnp.float32)  74.3 us
    scatter-add x4, other arithmetic, accumulate(): return (running.at[slot_ids].add(tile_sums), None)  42.3 us
    dot_general x12, matrix products, exact(): jnp.einsum(pattern, first_op, second_op, precision=lax.Precision.HIGHEST,...  35.2 us
    convert_element_type x6, local copies, waits for them, and re-layouts, local(): resid_grid.astype(jnp.bfloat16)  35.1 us
    all_to_all x2, blocking collectives, local(): lax.all_to_all(half_grid, 'vis', split_axis=3, concat_axis=2, tiled=True)  33.1 us
  transfers between devices with their start and end apart: 4, of which 4 were waited for; matrix products, arithmetic and copies ran while one was open for 0% of the time, Pallas kernels for 0%

commit v1 on v0

--- a/solution.py
+++ b/solution.py
@@ -119,7 +119,9 @@
         half_grid = jnp.stack([half_real, half_imag], axis=1).astype(jnp.bfloat16)
         column_half = lax.all_to_all(half_grid, "vis", split_axis=3, concat_axis=2, tiled=True)
         grid_part = column_pass(column_half, cosine_half, sine_half)
-        full_grid = lax.all_gather(grid_part, "vis", axis=3, tiled=True)
+        full_grid = jnp.concatenate(
+            lax.all_to_all(jnp.stack([grid_part] * lax.axis_size("vis")), "vis", 0, 0), axis=3
+        )
         patch_table = (
             full_grid.reshape(F, 2, P_SIZE // S, S, P_SIZE // S, S)
             .transpose(0, 2, 4, 1, 3, 5)

time: 1290 us -> 1080 us (0.84)
  waiting for transfers between devices: 950 us -> 693 us
  blocking collectives: 33.1 us -> 66.6 us
    all_gather x2 -> x0, waiting for transfers between devices: 307 us -> none  [local(): full_grid = lax.all_gather(grid_part, 'vis', axis=3, tiled=True)]
    all_to_all x0 -> x1, waiting for transfers between devices: none -> 47.2 us  [local(): lax.all_to_all(jnp.stack([grid_part] * lax.axis_size('vis')), 'vis', 0, 0)]
    all_to_all x0 -> x1, blocking collectives: none -> 33.4 us  [local(): lax.all_to_all(jnp.stack([grid_part] * lax.axis_size('vis')), 'vis', 0, 0)]
    another operation x2 -> x8, local copies, waits for them, and re-layouts: 7.8 us -> 25.1 us  [the longest x2 14.2 us: local(): full_grid.reshape(F, 2, P_SIZE // S, S, P_SIZE // S, S)]
  transfers between devices with their start and end apart: 4 -> 3, of which waited for: 4 -> 3; matrix products, arithmetic and copies ran while one was open for 0% -> 0% of each run, Pallas kernels for 0% -> 0%
where the time goes in v1:
time: 1080 us; the launch traced here: 1070 us
  waiting for transfers between devices  693 us (64%)
  local copies, waits for them, and re-layouts  125 us (12%)
  matrix products  114 us (11%)
  blocking collectives  66.6 us (6%)
  other arithmetic  51.4 us (5%)
  between operations  14.7 us (1%)
    psum x2, waiting for transfers between devices, local(): lax.psum(resid_grid.astype(jnp.bfloat16), 'vis').astype(jnp.float32)  646 us
    dot_general x76, matrix products, lowprec(): jnp.einsum(pattern, first_op, second_op, preferred_element_type=jnp.float32)  74.2 us
    all_to_all x1, waiting for transfers between devices, local(): lax.all_to_all(jnp.stack([grid_part] * lax.axis_size('vis')), 'vis', 0, 0)  47.2 us
    scatter-add x4, other arithmetic, accumulate(): return (running.at[slot_ids].add(tile_sums), None)  42.3 us
    dot_general x12, matrix products, exact(): jnp.einsum(pattern, first_op, second_op, precision=lax.Precision.HIGHEST,...  35.2 us
    convert_element_type x6, local copies, waits for them, and re-layouts, local(): resid_grid.astype(jnp.bfloat16)  35.1 us
    all_to_all x1, blocking collectives, local(): lax.all_to_all(jnp.stack([grid_part] * lax.axis_size('vis')), 'vis', 0, 0)  33.4 us
    all_to_all x2, blocking collectives, local(): lax.all_to_all(half_grid, 'vis', split_axis=3, concat_axis=2, tiled=True)  33.2 us
  transfers between devices with their start and end apart: 3, of which 3 were waited for; matrix products, arithmetic and copies ran while one was open for 0% of the time, Pallas kernels for 0%

profile of v1, /device:TPU:0, one launch (start us, length us, event | category | flops | bytes accessed | tf_op | source)
XLA Modules:
  0.0 1071.2 jit_solution(15086647585049936632)
XLA Ops:
  6.5 5.0 fusion.92
  11.6 4.2 fusion.95
  17.6 17.2 %all_to_all.46 = bf16[32,2,1024]{2,1,0:T(2,128)(2,1)S(1)} all-to-all(bf16[32,2,1024]{2,1,0:T(2,128)(2,1)S(1)} %reshape.195), channel_id=1, replica_groups=mesh['freq'=4,'vis'=32] {'vis'}, dimensions={0} | all-to-all | bytes 262144 | tf_op jit(solution)/shard_map/all_to_all | solution.py:120
  38.0 4.0 fusion.125
  42.0 4.0 fusion.127
  46.0 4.4 fusion.90
  50.4 4.2 fusion.91
  57.1 5.0 all-to-all-start.1
  65.3 47.2 %all-to-all-done.1 = bf16[32,4,2,512,16]{3,4,2,1,0:T(8,128)(2,1)} async-done(((bf16[32,4,2,512,16]{3,4,2,1,0:T(8,128)(2,1)}), bf16[32,4,2,512,16]{3,4,2,1,0:T(8,128)(2,1)}, u32[]{:S(2)}, u32[]{:S(2)}) %all-to-all-start.1) | async-done | bytes 4194336 | tf_op jit(solution)/shard_map/all_to_all | solution.py:123
  112.5 4.8 copy.120
  117.3 7.3 reshape_reshape.6
  124.6 7.5 copy.121
  132.1 7.3 reshape.161
  139.4 3.9 broadcast.78.clone
  143.3 42.9 %while.20 = (s32[]{:T(128)}, f32[64,32768]{1,0:T(8,128)}, s32[2,16]{1,0:T(2,128)S(1)}, s32[2,16]{1,0:T(2,128)S(1)}, bf16[16,32768]{1,0:T(8,128)(2,1)S(1)}, /*ind...) while((s32[]{:T(128)}, f32[64,32768]{1,0:T(8,128)}, ...), condition=%wide.region_2.3_spmd, body=%wide.region_0.2_spmd.sunk | while | flops 1164969216 | bytes 89130760 | solution.py:152
  154.1 10.6 scatter_custom_fusion.9
  175.5 10.6 scatter_custom_fusion.9
  186.2 4.0 convert_bitcast_fusion.1
  191.4 5.9 copy.183
  197.3 7.2 convert_element_type.195
  204.5 4.4 copy.124
  209.0 325.5 %all-reduce.3.cloned.1.call-done = bf16[4,2,512,512]{3,2,0,1:T(8,128)(2,1)} async-done(((bf16[4,2,512,512]{3,2,0,1:T(8,128)(2,1)}), bf16[4,2,512,512]{3,2,0,1:T(8,128)(2,1)}) %all-reduce.3.cloned.1.call-update) | async-done | bytes 4194320 | tf_op jit(solution)/shard_map/psum | solution.py:158
  534.5 2.8 fusion.63
  539.9 5.0 fusion.103
  547.1 4.7 fusion.81
  551.8 4.5 fusion.93
  556.3 4.5 fusion.94
  562.7 16.0 %all_to_all.47 = bf16[32,2,1024]{2,1,0:T(2,128)(2,1)S(1)} all-to-all(bf16[32,2,1024]{2,1,0:T(2,128)(2,1)S(1)} %reshape.197), channel_id=1, replica_groups=mesh['freq'=4,'vis'=32] {'vis'}, dimensions={0} | all-to-all | bytes 262144 | tf_op jit(solution)/shard_map/all_to_all | solution.py:120
  581.9 4.0 fusion.122
  585.9 4.0 fusion.120
  589.9 4.2 fusion.89
  594.1 4.2 fusion.88
  598.8 33.4 %all_to_all.48 = bf16[32,4,2,512,16]{3,4,2,1,0:T(8,128)(2,1)S(1)} all-to-all(bf16[32,4,2,512,16]{3,4,2,1,0:T(8,128)(2,1)S(1)} %stack.62), channel_id=1, replica_groups=mesh['freq'=4,'vis'=32] {'vis'}, dimensions={0} | all-to-all | bytes 8388608 | tf_op jit(solution)/shard_map/all_to_all | solution.py:123
  634.6 6.9 reshape_reshape.7
  641.6 7.5 copy.132
  649.0 7.3 reshape.163
  656.4 3.9 broadcast.78
  660.3 42.9 %while.21 = (s32[]{:T(128)}, f32[64,32768]{1,0:T(8,128)}, s32[2,16]{1,0:T(2,128)S(1)}, s32[2,16]{1,0:T(2,128)S(1)}, bf16[16,32768]{1,0:T(8,128)(2,1)S(1)}, /*ind...) while((s32[]{:T(128)}, f32[64,32768]{1,0:T(8,128)}, ...), condition=%wide.region_6.7_spmd, body=%wide.region_4.6_spmd.sunk | while | flops 1164969216 | bytes 89130760 | solution.py:152
  671.0 10.6 scatter_custom_fusion.11
  692.4 10.6 scatter_custom_fusion.11
  703.2 4.0 convert_bitcast_fusion
  708.4 5.9 copy.182
  714.3 7.2 convert_element_type.201
  721.5 4.4 copy.135
  725.9 320.2 %all-reduce.5.cloned.1.call-done = bf16[4,2,512,512]{3,2,0,1:T(8,128)(2,1)} async-done(((bf16[4,2,512,512]{3,2,0,1:T(8,128)(2,1)}), bf16[4,2,512,512]{3,2,0,1:T(8,128)(2,1)}) %all-reduce.5.cloned.1.call-update) | async-done | bytes 4194320 | tf_op jit(solution)/shard_map/psum | solution.py:158
  1046.1 2.8 fusion.67
  1051.5 4.7 fusion.101
  1058.5 5.6 fusion.72
  (166 shorter events, 72.4 us)
Async XLA Ops:
  6.5 5.1 copy-start.6
  57.1 5.1 copy-start.4
  57.1 55.4 %all-to-all-start.1 = ((bf16[32,4,2,512,16]{3,4,2,1,0:T(8,128)(2,1)}), bf16[32,4,2,512,16]{3,4,2,1,0:T(8,128)(2,1)}, u32[]{:S(2)}, u32[]{:S(2)}) async-start(bf16[32,4,2,512,16]{3,4,2,1,0:T(8,128)(2,1)} %stack.55), calls=%async_computation.1 | async-start | bytes 8388608 | tf_op jit(solution)/shard_map/all_to_all | solution.py:123
  62.1 3.0 copy-start.7
  62.1 3.0 copy-start.8
  62.1 3.1 copy-start.9
  62.1 472.4 %all-reduce.3.cloned.1.call-start = ((), (), s32[]{:S(2)}) async-start(), calls=%async_computation.4 | async-start | bytes 8388608 | tf_op jit(solution)/shard_map/psum | solution.py:158
  62.2 1.6 copy-start.5
  143.3 2.2 copy-start.1
  164.7 2.2 copy-start.1
  209.0 837.1 %all-reduce.5.cloned.1.call-start = ((), (), s32[]{:S(2)}) async-start(), calls=%async_computation.5 | async-start | bytes 8388608 | tf_op jit(solution)/shard_map/psum | solution.py:158
  534.5 10.4 copy-start.2
  660.3 2.2 copy-start
  681.6 2.2 copy-start
  1046.1 10.2 copy-start.3
Sparse Core Ops, SparseCore 0:
  209.1 325.3 all-reduce.2
  726.1 319.9 all-reduce.4
